TPU v7x, 32 devices: a whole 2x2x4 slice. The times are simulated.
32 devices in a mesh: row: 4 (over z), col: 8 (over y, x, core).
Axes of the slice: x: 2, y: 2, z: 4, core: 2. Of those that a mesh axis runs over, the one named last changes fastest.
Arguments:
- root_factor: float32 [2, 4, 2560, 20480], P(None, 'row', None, 'col'), may hold values from -0.0390625 to 0.0390625
- root_rhs: float32 [20480, 64], P('col'), may hold values from -6 to 6
- child_factor: float32 [8, 4096, 4096], P('col', 'row'), may hold values from -0.09375 to 0.09375
- child_rhs: float32 [8, 4096, 64], P('col', 'row'), may hold values from -6 to 6
- child_map: int32 [8, 4096], P('col'), may hold values from 0 to 20479, as said below
Outputs:
- root_solution: float32 [20480, 64], P('col')
- child_solution: float32 [8, 4096, 64], P('col', 'row')
Inputs may be any that keep to these rules, and one draw needn't show every extreme that they name: Each row of child_map is strictly increasing; its entries at positions j * 512 to (j + 1) * 512 - 1 lie in root rows j * 2560 to (j + 1) * 2560 - 1.
All inputs are finite; a program needn't handle non-finite values.
Results may differ from a plain program's by a relative error of at most 0.0001.
Values sent between devices are 32-bit elements; how exact they have to be, the bound alone decides.
No kernel may reach another device: no remote copies, remote signals or barrier semaphores. Data moves between devices by JAX's collectives and lax.ppermute only.
A program may use at most 128 MiB of HBM per device.

v0:
```python
import jax
import jax.numpy as jnp
from jax import lax
from jax.sharding import PartitionSpec as P


def spread(block, axis, source):
    block = jnp.where(lax.axis_index(axis) == source, block, jnp.zeros_like(block))
    return lax.psum(block, axis)


def spread_panel(partial_value, owner_row):
    summed = lax.psum(partial_value, "col")
    return spread(summed, "row", owner_row)


def solve_panel(panel_id, solved, blocks, root_rhs, global_rows):
    row_count = lax.axis_size("row")
    block_slot = panel_id // row_count
    owner_row = panel_id % row_count
    panel_rows = lax.dynamic_index_in_dim(blocks, block_slot, 0, keepdims=False)
    partial_value = jnp.dot(
        panel_rows, solved, precision=lax.Precision.HIGHEST, preferred_element_type=jnp.float32
    )
    summed = spread_panel(partial_value, owner_row)
    panel_size = panel_rows.shape[0]
    offset = global_rows - panel_id * panel_size
    inside = (offset >= 0) & (offset < panel_size)
    picked = jnp.take(summed, jnp.clip(offset, 0, panel_size - 1), axis=0)
    return jnp.where(inside[:, None], root_rhs - picked, solved)


def body(root_factor, root_rhs, child_factor, child_rhs, child_map):
    blocks = root_factor[:, 0]
    own_rows = blocks.shape[2]
    panel_count = blocks.shape[0] * lax.axis_size("row")
    col_id = lax.axis_index("col")
    global_rows = col_id * own_rows + jnp.arange(own_rows, dtype=jnp.int32)

    def advance(turn, solved):
        upper = panel_count - 1 - 2 * turn
        solved = solve_panel(upper, solved, blocks, root_rhs, global_rows)
        return solve_panel(upper - 1, solved, blocks, root_rhs, global_rows)

    solved = lax.fori_loop(0, panel_count // 2, advance, jnp.zeros(root_rhs.shape, jnp.float32))
    child_block = child_factor[0]
    row_map = child_map[0]
    col_count = lax.axis_size("col")
    per_owner = row_map.shape[0] // col_count
    wanted = row_map.reshape(col_count, per_owner)
    asked = lax.all_to_all(wanted, "col", split_axis=0, concat_axis=0, tiled=True)
    served = jnp.take(solved, asked - col_id * own_rows, axis=0)
    parent_rows = lax.all_to_all(served, "col", split_axis=0, concat_axis=0, tiled=True)
    coupled = jnp.dot(
        child_block,
        parent_rows.reshape(row_map.shape[0], solved.shape[1]),
        precision=lax.Precision.HIGHEST,
        preferred_element_type=jnp.float32,
    )
    child_solution = child_rhs - coupled[None]
    return (solved, child_solution)


def solution(mesh):
    return jax.shard_map(
        body,
        mesh=mesh,
        in_specs=(
            P(None, "row", None, "col"),
            P("col", None),
            P("col", "row", None),
            P("col", "row", None),
            P("col", None),
        ),
        out_specs=(P("col", None), P("col", "row", None)),
        check_vma=False,
    )
```

profile of v0, /device:TPU:0, one launch (start us, length us, event | category | flops | bytes accessed | tf_op | source)
XLA Modules:
  0.0 1184.0 jit_solution(4137197244036961348)
XLA Ops:
  7.2 5.2 all-to-all-start
  12.4 2.6 copy.18
  15.0 2.2 all-to-all-done
  17.2 1106.1 %while.19 = (s32[]{:T(128)}, f32[2560,64]{1,0:T(8,128)S(1)}, f32[2,2560,2560]{2,1,0:T(8,128)}, f32[2560,64]{1,0:T(8,128)}, s32[]{:T(128)}, /*index=5*/s32[]{:T(1...) while((s32[]{:T(128)}, f32[2560,64]{1,0:T(8,128)S(1)}, ...), condition=%wide.region_5.7_spmd.clone, body=%wide.region_0.6_spmd.clone.sunk | while | flops 10069377024 | bytes 84653952 | solution.py:45
  17.3 29.3 %fusion.49 = f32[2560,64]{0,1:T(8,128)} fusion(f32[2,2560,2560]{2,1,0:T(8,128)} %get-tuple-element.329, s32[]{:T(128)S(6)} %select_n.295, f32[2560,64]{1,0:T(8,128)S(1)} %get-tuple-element.313, pred[]{:T(512)S(6)} %compare.37), kind=kOutput, calls=%fused_computation.4.clone.1 | convolution fusion | flops 5033328640 | bytes 27525124 | tf_op jit(solution)/shard_map/while/body/eval_jaxpr/dot_general | solution.py:22
  46.7 54.9 %all-reduce.5.cloned.1.call-done = f32[2560,64]{0,1:T(8,128)} async-done(((f32[2560,64]{0,1:T(8,128)}), f32[2560,64]{0,1:T(8,128)}) %all-reduce.5.cloned.1.call-update) | async-done | bytes 655376 | tf_op jit(solution)/shard_map/while/body/eval_jaxpr/psum | solution.py:13
  101.6 0.9 broadcast_select_fusion.5
  102.6 41.8 %all-reduce.7.cloned.1.call-done = f32[2560,64]{0,1:T(8,128)} async-done(((f32[2560,64]{0,1:T(8,128)}), f32[2560,64]{0,1:T(8,128)}) %all-reduce.7.cloned.1.call-update) | async-done | bytes 655376 | tf_op jit(solution)/shard_map/while/body/eval_jaxpr/psum | solution.py:9
  144.4 1.5 copy.29
  145.9 5.6 gather_fusion
  151.5 31.5 %fusion.51 = f32[2560,64]{0,1:T(8,128)} fusion(f32[2,2560,2560]{2,1,0:T(8,128)} %get-tuple-element.329, s32[]{:T(128)S(6)} %select_n.293, f32[2560,64]{1,0:T(8,128)} %get-tuple-element.330, f32[2560,64]{1,0:T(8,128)} %gather_fusion, f32[2560,64]{1,0:T(8,128)S(1)} %get-tuple-element.313, pred[2560]{0:T(1024)(128)(4,1)S(1)} %get-tuple-element.293, ...), kind=kOutput, calls=%fused_computation.6.clone.1 | convolution fusion | flops 5033820160 | bytes 30151684 | tf_op jit(solution)/shard_map/while/body/eval_jaxpr/dot_general | solution.py:22
  183.1 54.8 %all-reduce.9.cloned.1.call-done = f32[2560,64]{0,1:T(8,128)} async-done(((f32[2560,64]{0,1:T(8,128)}), f32[2560,64]{0,1:T(8,128)}) %all-reduce.9.cloned.1.call-update) | async-done | bytes 655376 | tf_op jit(solution)/shard_map/while/body/eval_jaxpr/psum | solution.py:13
  238.0 0.9 broadcast_select_fusion.6
  238.9 41.7 %all-reduce.11.cloned.1.call-done = f32[2560,64]{0,1:T(8,128)} async-done(((f32[2560,64]{0,1:T(8,128)}), f32[2560,64]{0,1:T(8,128)}) %all-reduce.11.cloned.1.call-update) | async-done | bytes 655376 | tf_op jit(solution)/shard_map/while/body/eval_jaxpr/psum | solution.py:9
  280.7 1.5 copy.30
  282.1 5.6 gather_fusion.1
  287.8 6.0 fusion.53
  293.9 29.3 %fusion.49 = f32[2560,64]{0,1:T(8,128)} fusion(f32[2,2560,2560]{2,1,0:T(8,128)} %get-tuple-element.329, s32[]{:T(128)S(6)} %select_n.295, f32[2560,64]{1,0:T(8,128)S(1)} %get-tuple-element.313, pred[]{:T(512)S(6)} %compare.37), kind=kOutput, calls=%fused_computation.4.clone.1 | convolution fusion | flops 5033328640 | bytes 27525124 | tf_op jit(solution)/shard_map/while/body/eval_jaxpr/dot_general | solution.py:22
  323.3 54.9 %all-reduce.5.cloned.1.call-done = f32[2560,64]{0,1:T(8,128)} async-done(((f32[2560,64]{0,1:T(8,128)}), f32[2560,64]{0,1:T(8,128)}) %all-reduce.5.cloned.1.call-update) | async-done | bytes 655376 | tf_op jit(solution)/shard_map/while/body/eval_jaxpr/psum | solution.py:13
  378.1 0.9 broadcast_select_fusion.5
  379.2 41.7 %all-reduce.7.cloned.1.call-done = f32[2560,64]{0,1:T(8,128)} async-done(((f32[2560,64]{0,1:T(8,128)}), f32[2560,64]{0,1:T(8,128)}) %all-reduce.7.cloned.1.call-update) | async-done | bytes 655376 | tf_op jit(solution)/shard_map/while/body/eval_jaxpr/psum | solution.py:9
  420.8 1.5 copy.29
  422.3 5.6 gather_fusion
  427.9 31.5 %fusion.51 = f32[2560,64]{0,1:T(8,128)} fusion(f32[2,2560,2560]{2,1,0:T(8,128)} %get-tuple-element.329, s32[]{:T(128)S(6)} %select_n.293, f32[2560,64]{1,0:T(8,128)} %get-tuple-element.330, f32[2560,64]{1,0:T(8,128)} %gather_fusion, f32[2560,64]{1,0:T(8,128)S(1)} %get-tuple-element.313, pred[2560]{0:T(1024)(128)(4,1)S(1)} %get-tuple-element.293, ...), kind=kOutput, calls=%fused_computation.6.clone.1 | convolution fusion | flops 5033820160 | bytes 30151684 | tf_op jit(solution)/shard_map/while/body/eval_jaxpr/dot_general | solution.py:22
  459.6 54.8 %all-reduce.9.cloned.1.call-done = f32[2560,64]{0,1:T(8,128)} async-done(((f32[2560,64]{0,1:T(8,128)}), f32[2560,64]{0,1:T(8,128)}) %all-reduce.9.cloned.1.call-update) | async-done | bytes 655376 | tf_op jit(solution)/shard_map/while/body/eval_jaxpr/psum | solution.py:13
  514.4 2.0 broadcast_select_fusion.6
  516.5 40.8 %all-reduce.11.cloned.1.call-done = f32[2560,64]{0,1:T(8,128)} async-done(((f32[2560,64]{0,1:T(8,128)}), f32[2560,64]{0,1:T(8,128)}) %all-reduce.11.cloned.1.call-update) | async-done | bytes 655376 | tf_op jit(solution)/shard_map/while/body/eval_jaxpr/psum | solution.py:9
  557.2 1.5 copy.30
  558.7 5.6 gather_fusion.1
  564.3 6.0 fusion.53
  570.5 29.3 %fusion.49 = f32[2560,64]{0,1:T(8,128)} fusion(f32[2,2560,2560]{2,1,0:T(8,128)} %get-tuple-element.329, s32[]{:T(128)S(6)} %select_n.295, f32[2560,64]{1,0:T(8,128)S(1)} %get-tuple-element.313, pred[]{:T(512)S(6)} %compare.37), kind=kOutput, calls=%fused_computation.4.clone.1 | convolution fusion | flops 5033328640 | bytes 27525124 | tf_op jit(solution)/shard_map/while/body/eval_jaxpr/dot_general | solution.py:22
  599.9 54.9 %all-reduce.5.cloned.1.call-done = f32[2560,64]{0,1:T(8,128)} async-done(((f32[2560,64]{0,1:T(8,128)}), f32[2560,64]{0,1:T(8,128)}) %all-reduce.5.cloned.1.call-update) | async-done | bytes 655376 | tf_op jit(solution)/shard_map/while/body/eval_jaxpr/psum | solution.py:13
  654.7 0.9 broadcast_select_fusion.5
  655.8 41.6 %all-reduce.7.cloned.1.call-done = f32[2560,64]{0,1:T(8,128)} async-done(((f32[2560,64]{0,1:T(8,128)}), f32[2560,64]{0,1:T(8,128)}) %all-reduce.7.cloned.1.call-update) | async-done | bytes 655376 | tf_op jit(solution)/shard_map/while/body/eval_jaxpr/psum | solution.py:9
  697.4 1.5 copy.29
  698.9 5.6 gather_fusion
  704.5 31.5 %fusion.51 = f32[2560,64]{0,1:T(8,128)} fusion(f32[2,2560,2560]{2,1,0:T(8,128)} %get-tuple-element.329, s32[]{:T(128)S(6)} %select_n.293, f32[2560,64]{1,0:T(8,128)} %get-tuple-element.330, f32[2560,64]{1,0:T(8,128)} %gather_fusion, f32[2560,64]{1,0:T(8,128)S(1)} %get-tuple-element.313, pred[2560]{0:T(1024)(128)(4,1)S(1)} %get-tuple-element.293, ...), kind=kOutput, calls=%fused_computation.6.clone.1 | convolution fusion | flops 5033820160 | bytes 30151684 | tf_op jit(solution)/shard_map/while/body/eval_jaxpr/dot_general | solution.py:22
  736.1 54.8 %all-reduce.9.cloned.1.call-done = f32[2560,64]{0,1:T(8,128)} async-done(((f32[2560,64]{0,1:T(8,128)}), f32[2560,64]{0,1:T(8,128)}) %all-reduce.9.cloned.1.call-update) | async-done | bytes 655376 | tf_op jit(solution)/shard_map/while/body/eval_jaxpr/psum | solution.py:13
  791.0 0.9 broadcast_select_fusion.6
  791.9 41.7 %all-reduce.11.cloned.1.call-done = f32[2560,64]{0,1:T(8,128)} async-done(((f32[2560,64]{0,1:T(8,128)}), f32[2560,64]{0,1:T(8,128)}) %all-reduce.11.cloned.1.call-update) | async-done | bytes 655376 | tf_op jit(solution)/shard_map/while/body/eval_jaxpr/psum | solution.py:9
  833.7 1.5 copy.30
  835.2 5.6 gather_fusion.1
  840.8 6.0 fusion.53
  846.9 29.3 %fusion.49 = f32[2560,64]{0,1:T(8,128)} fusion(f32[2,2560,2560]{2,1,0:T(8,128)} %get-tuple-element.329, s32[]{:T(128)S(6)} %select_n.295, f32[2560,64]{1,0:T(8,128)S(1)} %get-tuple-element.313, pred[]{:T(512)S(6)} %compare.37), kind=kOutput, calls=%fused_computation.4.clone.1 | convolution fusion | flops 5033328640 | bytes 27525124 | tf_op jit(solution)/shard_map/while/body/eval_jaxpr/dot_general | solution.py:22
  876.3 54.9 %all-reduce.5.cloned.1.call-done = f32[2560,64]{0,1:T(8,128)} async-done(((f32[2560,64]{0,1:T(8,128)}), f32[2560,64]{0,1:T(8,128)}) %all-reduce.5.cloned.1.call-update) | async-done | bytes 655376 | tf_op jit(solution)/shard_map/while/body/eval_jaxpr/psum | solution.py:13
  931.2 0.9 broadcast_select_fusion.5
  932.2 41.7 %all-reduce.7.cloned.1.call-done = f32[2560,64]{0,1:T(8,128)} async-done(((f32[2560,64]{0,1:T(8,128)}), f32[2560,64]{0,1:T(8,128)}) %all-reduce.7.cloned.1.call-update) | async-done | bytes 655376 | tf_op jit(solution)/shard_map/while/body/eval_jaxpr/psum | solution.py:9
  973.9 1.5 copy.29
  975.3 5.6 gather_fusion
  981.0 31.5 %fusion.51 = f32[2560,64]{0,1:T(8,128)} fusion(f32[2,2560,2560]{2,1,0:T(8,128)} %get-tuple-element.329, s32[]{:T(128)S(6)} %select_n.293, f32[2560,64]{1,0:T(8,128)} %get-tuple-element.330, f32[2560,64]{1,0:T(8,128)} %gather_fusion, f32[2560,64]{1,0:T(8,128)S(1)} %get-tuple-element.313, pred[2560]{0:T(1024)(128)(4,1)S(1)} %get-tuple-element.293, ...), kind=kOutput, calls=%fused_computation.6.clone.1 | convolution fusion | flops 5033820160 | bytes 30151684 | tf_op jit(solution)/shard_map/while/body/eval_jaxpr/dot_general | solution.py:22
  1012.6 54.8 %all-reduce.9.cloned.1.call-done = f32[2560,64]{0,1:T(8,128)} async-done(((f32[2560,64]{0,1:T(8,128)}), f32[2560,64]{0,1:T(8,128)}) %all-reduce.9.cloned.1.call-update) | async-done | bytes 655376 | tf_op jit(solution)/shard_map/while/body/eval_jaxpr/psum | solution.py:13
  1067.4 2.0 broadcast_select_fusion.6
  1069.5 40.6 %all-reduce.11.cloned.1.call-done = f32[2560,64]{0,1:T(8,128)} async-done(((f32[2560,64]{0,1:T(8,128)}), f32[2560,64]{0,1:T(8,128)}) %all-reduce.11.cloned.1.call-update) | async-done | bytes 655376 | tf_op jit(solution)/shard_map/while/body/eval_jaxpr/psum | solution.py:9
  1110.1 1.5 copy.30
  1111.6 5.6 gather_fusion.1
  1117.2 6.0 fusion.53
  1123.2 11.0 gather_fusion.2
  1134.2 1.6 copy.19
  1135.8 2.3 broadcast_select_fusion.2
  1138.1 3.7 all-to-all-start.1
  1141.8 1.2 copy.21
  1143.0 14.2 %all-to-all-done.1 = f32[8,512,64]{1,2,0:T(8,128)S(1)} async-done(((f32[8,512,64]{1,2,0:T(8,128)}), f32[8,512,64]{1,2,0:T(8,128)S(1)}, u32[]{:S(2)}, u32[]{:S(2)}) %all-to-all-start.1) | async-done | bytes 1048608 | tf_op jit(solution)/shard_map/all_to_all | solution.py:53
  1157.1 0.1 copy.23
  1157.2 20.2 %fusion.32 = f32[1,1024,64]{1,2,0:T(8,128)} fusion(f32[1,1024,64]{1,2,0:T(8,128)S(1)} %copy-done, f32[4096,64]{0,1:T(8,128)S(1)} %bitcast.38, f32[1,1024,4096]{2,1,0:T(8,128)} %param.11), kind=kOutput, calls=%fused_computation.42 | convolution fusion | flops 3221291008 | bytes 18350080 | tf_op jit(solution)/shard_map/dot_general | solution.py:54
  (62 shorter events, 1.3 us)
Async XLA Ops:
  7.2 10.0 all-to-all-start
  17.2 84.4 %all-reduce.5.cloned.1.call-start = ((), (), s32[]{:S(2)}) async-start(), calls=%async_computation.2 | async-start | bytes 1310720 | tf_op jit(solution)/shard_map/while/body/eval_jaxpr/psum | solution.py:13
  46.6 97.8 %all-reduce.7.cloned.1.call-start = ((), (), s32[]{:S(2)}) async-start(), calls=%async_computation.3 | async-start | bytes 1310720 | tf_op jit(solution)/shard_map/while/body/eval_jaxpr/psum | solution.py:9
  102.5 135.5 %all-reduce.9.cloned.1.call-start = ((), (), s32[]{:S(2)}) async-start(), calls=%async_computation.4 | async-start | bytes 1310720 | tf_op jit(solution)/shard_map/while/body/eval_jaxpr/psum | solution.py:13
  183.0 97.6 %all-reduce.11.cloned.1.call-start = ((), (), s32[]{:S(2)}) async-start(), calls=%async_computation.5 | async-start | bytes 1310720 | tf_op jit(solution)/shard_map/while/body/eval_jaxpr/psum | solution.py:9
  293.8 84.4 %all-reduce.5.cloned.1.call-start = ((), (), s32[]{:S(2)}) async-start(), calls=%async_computation.2 | async-start | bytes 1310720 | tf_op jit(solution)/shard_map/while/body/eval_jaxpr/psum | solution.py:13
  323.2 97.6 %all-reduce.7.cloned.1.call-start = ((), (), s32[]{:S(2)}) async-start(), calls=%async_computation.3 | async-start | bytes 1310720 | tf_op jit(solution)/shard_map/while/body/eval_jaxpr/psum | solution.py:9
  379.1 135.3 %all-reduce.9.cloned.1.call-start = ((), (), s32[]{:S(2)}) async-start(), calls=%async_computation.4 | async-start | bytes 1310720 | tf_op jit(solution)/shard_map/while/body/eval_jaxpr/psum | solution.py:13
  459.5 97.7 %all-reduce.11.cloned.1.call-start = ((), (), s32[]{:S(2)}) async-start(), calls=%async_computation.5 | async-start | bytes 1310720 | tf_op jit(solution)/shard_map/while/body/eval_jaxpr/psum | solution.py:9
  570.4 84.3 %all-reduce.5.cloned.1.call-start = ((), (), s32[]{:S(2)}) async-start(), calls=%async_computation.2 | async-start | bytes 1310720 | tf_op jit(solution)/shard_map/while/body/eval_jaxpr/psum | solution.py:13
  599.8 97.6 %all-reduce.7.cloned.1.call-start = ((), (), s32[]{:S(2)}) async-start(), calls=%async_computation.3 | async-start | bytes 1310720 | tf_op jit(solution)/shard_map/while/body/eval_jaxpr/psum | solution.py:9
  655.6 135.3 %all-reduce.9.cloned.1.call-start = ((), (), s32[]{:S(2)}) async-start(), calls=%async_computation.4 | async-start | bytes 1310720 | tf_op jit(solution)/shard_map/while/body/eval_jaxpr/psum | solution.py:13
  736.0 97.6 %all-reduce.11.cloned.1.call-start = ((), (), s32[]{:S(2)}) async-start(), calls=%async_computation.5 | async-start | bytes 1310720 | tf_op jit(solution)/shard_map/while/body/eval_jaxpr/psum | solution.py:9
  846.8 84.4 %all-reduce.5.cloned.1.call-start = ((), (), s32[]{:S(2)}) async-start(), calls=%async_computation.2 | async-start | bytes 1310720 | tf_op jit(solution)/shard_map/while/body/eval_jaxpr/psum | solution.py:13
  876.2 97.6 %all-reduce.7.cloned.1.call-start = ((), (), s32[]{:S(2)}) async-start(), calls=%async_computation.3 | async-start | bytes 1310720 | tf_op jit(solution)/shard_map/while/body/eval_jaxpr/psum | solution.py:9
  932.1 135.3 %all-reduce.9.cloned.1.call-start = ((), (), s32[]{:S(2)}) async-start(), calls=%async_computation.4 | async-start | bytes 1310720 | tf_op jit(solution)/shard_map/while/body/eval_jaxpr/psum | solution.py:13
  1012.5 97.6 %all-reduce.11.cloned.1.call-start = ((), (), s32[]{:S(2)}) async-start(), calls=%async_computation.5 | async-start | bytes 1310720 | tf_op jit(solution)/shard_map/while/body/eval_jaxpr/psum | solution.py:9
  1138.1 19.0 %all-to-all-start.1 = ((f32[8,512,64]{1,2,0:T(8,128)}), f32[8,512,64]{1,2,0:T(8,128)S(1)}, u32[]{:S(2)}, u32[]{:S(2)}) async-start(f32[8,512,64]{1,2,0:T(8,128)} %broadcast_select_fusion.2), calls=%async_computation.1 | async-start | bytes 2097152 | tf_op jit(solution)/shard_map/all_to_all | solution.py:53
  1143.0 14.2 %copy-start = (f32[1,1024,64]{1,2,0:T(8,128)S(1)}, f32[1,1024,64]{1,2,0:T(8,128)}, u32[]{:S(2)}) copy-start(f32[1,1024,64]{1,2,0:T(8,128)} %param.12) | copy-start | bytes 786436
Sparse Core Ops, SparseCore 0:
  46.7 54.7 all-reduce.4
  104.5 39.8 all-reduce.6
  183.2 54.7 all-reduce.8
  240.7 39.8 all-reduce.10
  323.3 54.7 all-reduce.4
  380.9 39.8 all-reduce.6
  459.6 54.7 all-reduce.8
  517.3 39.8 all-reduce.10
  599.9 54.7 all-reduce.4
  657.5 39.8 all-reduce.6
  736.2 54.7 all-reduce.8
  793.8 39.8 all-reduce.10
  876.3 54.7 all-reduce.4
  933.9 39.8 all-reduce.6
  1012.6 54.7 all-reduce.8
  1070.2 39.8 all-reduce.10
where the time goes:
time: 1190 us; the launch traced here: 1180 us
  waiting for transfers between devices  787 us (66%)
  matrix products  264 us (22%)
  local copies, waits for them, and re-layouts  73.1 us (6%)
  other arithmetic  36 us (3%)
  between operations  13.7 us (1%)
    psum x8, waiting for transfers between devices, spread_panel(): summed = lax.psum(partial_value, 'col')  439 us
    psum x8, waiting for transfers between devices, spread(): return lax.psum(block, axis)  332 us
    dot_general x8, matrix products, solve_panel(): jnp.dot(panel_rows, solved, precision=lax.Precision.HIGHEST, preferred_el...  243 us
    gather x8, local copies, waits for them, and re-layouts, solve_panel(): picked = jnp.take(summed, jnp.clip(offset, 0, panel_size - 1), axis=0)  44.9 us
    select_n x4, other arithmetic, solve_panel(): return jnp.where(inside[:, None], root_rhs - picked, solved)  24 us
  transfers between devices with their start and end apart: 18, of which 18 were waited for; matrix products, arithmetic and copies ran while one was open for 0% of the time, Pallas kernels for 0%

commit v1 on v0

--- a/solution.py
+++ b/solution.py
@@ -10,7 +10,8 @@
 
 
 def spread_panel(partial_value, owner_row):
-    summed = lax.psum(partial_value, "col")
+    obtain_shapes = lambda values: jnp.sum(jax.lax.all_gather(values, "col"), 0)
+    summed = obtain_shapes(partial_value)
     return spread(summed, "row", owner_row)
 
 

time: 1190 us -> 1280 us (1.076)
  local copies, waits for them, and re-layouts: 73.1 us -> 117 us
  waiting for transfers between devices: 787 us -> 821 us
  other arithmetic: 36 us -> 49.1 us
    psum x8 -> x0, waiting for transfers between devices: 439 us -> none  [spread_panel(): summed = lax.psum(partial_value, 'col')]
    all_gather x0 -> x8, waiting for transfers between devices: none -> 325 us  [spread_panel(): obtain_shapes = lambda values: jnp.sum(jax.lax.all_gather(values, 'col'), 0)]
    psum x8, waiting for transfers between devices: 332 us -> 479 us  [spread(): return lax.psum(block, axis)]
    while x0 -> x8, local copies, waits for them, and re-layouts: none -> 43.6 us
where the time goes in v1:
time: 1280 us
  waiting for transfers between devices  821 us (64%)
  matrix products  267 us (21%)
  local copies, waits for them, and re-layouts  117 us (9%)
  other arithmetic  49.1 us (4%)
  between operations  13.8 us (1%)
    psum x8, waiting for transfers between devices, spread(): return lax.psum(block, axis)  479 us
    all_gather x8, waiting for transfers between devices, spread_panel(): obtain_shapes = lambda values: jnp.sum(jax.lax.all_gather(values, 'col'), 0)  325 us
    dot_general x8, matrix products, solve_panel(): jnp.dot(panel_rows, solved, precision=lax.Precision.HIGHEST, preferred_el...  247 us
    gather x8, local copies, waits for them, and re-layouts, solve_panel(): picked = jnp.take(summed, jnp.clip(offset, 0, panel_size - 1), axis=0)  49.5 us
    while x8, local copies, waits for them, and re-layouts  43.6 us
  transfers between devices with their start and end apart: 18, of which 18 were waited for; matrix products, arithmetic and copies ran while one was open for 0% of the time, Pallas kernels for 0%

profile of v1, /device:TPU:0, one launch (start us, length us, event | category | flops | bytes accessed | tf_op | source)
XLA Modules:
  0.0 1278.1 jit_solution(2389579704801774783)
XLA Ops:
  7.2 5.2 all-to-all-start
  12.4 2.6 copy.16
  15.0 2.2 all-to-all-done
  18.4 1199.2 %while.19 = (s32[]{:T(128)}, f32[2560,64]{1,0:T(8,128)S(1)}, f32[2,2560,2560]{2,1,0:T(8,128)}, f32[2560,64]{1,0:T(8,128)}, s32[]{:T(128)}, /*index=5*/s32[]{:T(1...) while((s32[]{:T(128)}, f32[2560,64]{1,0:T(8,128)S(1)}, ...), condition=%wide.region_5.7_spmd.clone, body=%wide.region_0.6_spmd.clone.sunk | while | flops 10071343104 | bytes 146913200 | solution.py:46
  18.4 29.3 %fusion.49 = f32[2560,64]{0,1:T(8,128)} fusion(f32[2,2560,2560]{2,1,0:T(8,128)} %get-tuple-element.329, s32[]{:T(128)S(6)} %select_n.295, f32[2560,64]{1,0:T(8,128)S(1)} %get-tuple-element.313, pred[]{:T(512)S(6)} %compare.37), kind=kOutput, calls=%fused_computation.4.clone.1 | convolution fusion | flops 5033328640 | bytes 27525124 | tf_op jit(solution)/shard_map/while/body/eval_jaxpr/dot_general | solution.py:23
  47.8 40.6 %all-gather.11.cloned.1.call-done = f32[20480,64]{0,1:T(8,128)} async-done(((f32[2560,64]{0,1:T(8,128)}), f32[20480,64]{0,1:T(8,128)}) %all-gather.11.cloned.1.call-update) | async-done | bytes 5242896 | tf_op jit(solution)/shard_map/while/body/eval_jaxpr/all_gather | solution.py:13
  88.4 5.4 copy.31
  93.9 1.3 bitcast_reduce_fusion.4
  96.9 60.1 %all-reduce.3.cloned.1.call-done = f32[2560,64]{1,0:T(8,128)} async-done(((f32[2560,64]{1,0:T(8,128)}), f32[2560,64]{1,0:T(8,128)}) %all-reduce.3.cloned.1.call-update) | async-done | bytes 655376 | tf_op jit(solution)/shard_map/while/body/eval_jaxpr/psum | solution.py:9
  157.0 5.5 gather_fusion
  162.5 32.3 %fusion.51 = f32[2560,64]{0,1:T(8,128)} fusion(f32[2,2560,2560]{2,1,0:T(8,128)} %get-tuple-element.329, s32[]{:T(128)S(6)} %select_n.293, f32[2560,64]{1,0:T(8,128)} %get-tuple-element.330, f32[2560,64]{1,0:T(8,128)S(1)} %gather_fusion, f32[2560,64]{1,0:T(8,128)S(1)} %get-tuple-element.313, pred[2560]{0:T(1024)(128)(4,1)S(1)} %get-tuple-element.293, ...), kind=kOutput, calls=%fused_computation.6.clone.1 | convolution fusion | flops 5033820160 | bytes 29496324 | tf_op jit(solution)/shard_map/while/body/eval_jaxpr/dot_general | solution.py:23
  194.9 40.6 %all-gather.13.cloned.1.call-done = f32[20480,64]{0,1:T(8,128)} async-done(((f32[2560,64]{0,1:T(8,128)}), f32[20480,64]{0,1:T(8,128)}) %all-gather.13.cloned.1.call-update) | async-done | bytes 5242896 | tf_op jit(solution)/shard_map/while/body/eval_jaxpr/all_gather | solution.py:13
  235.5 5.4 copy.33
  241.0 1.3 bitcast_reduce_fusion.5
  242.3 1.5 copy.34
  245.0 60.6 %all-reduce.5.cloned.1.call-done = f32[2560,64]{1,0:T(8,128)} async-done(((f32[2560,64]{1,0:T(8,128)}), f32[2560,64]{1,0:T(8,128)}) %all-reduce.5.cloned.1.call-update) | async-done | bytes 655376 | tf_op jit(solution)/shard_map/while/body/eval_jaxpr/psum | solution.py:9
  305.5 6.9 gather_fusion.1
  312.5 5.7 fusion.53
  318.3 29.3 %fusion.49 = f32[2560,64]{0,1:T(8,128)} fusion(f32[2,2560,2560]{2,1,0:T(8,128)} %get-tuple-element.329, s32[]{:T(128)S(6)} %select_n.295, f32[2560,64]{1,0:T(8,128)S(1)} %get-tuple-element.313, pred[]{:T(512)S(6)} %compare.37), kind=kOutput, calls=%fused_computation.4.clone.1 | convolution fusion | flops 5033328640 | bytes 27525124 | tf_op jit(solution)/shard_map/while/body/eval_jaxpr/dot_general | solution.py:23
  347.7 40.6 %all-gather.11.cloned.1.call-done = f32[20480,64]{0,1:T(8,128)} async-done(((f32[2560,64]{0,1:T(8,128)}), f32[20480,64]{0,1:T(8,128)}) %all-gather.11.cloned.1.call-update) | async-done | bytes 5242896 | tf_op jit(solution)/shard_map/while/body/eval_jaxpr/all_gather | solution.py:13
  388.3 5.4 copy.31
  393.8 1.3 bitcast_reduce_fusion.4
  396.8 60.1 %all-reduce.3.cloned.1.call-done = f32[2560,64]{1,0:T(8,128)} async-done(((f32[2560,64]{1,0:T(8,128)}), f32[2560,64]{1,0:T(8,128)}) %all-reduce.3.cloned.1.call-update) | async-done | bytes 655376 | tf_op jit(solution)/shard_map/while/body/eval_jaxpr/psum | solution.py:9
  456.9 5.5 gather_fusion
  462.4 32.3 %fusion.51 = f32[2560,64]{0,1:T(8,128)} fusion(f32[2,2560,2560]{2,1,0:T(8,128)} %get-tuple-element.329, s32[]{:T(128)S(6)} %select_n.293, f32[2560,64]{1,0:T(8,128)} %get-tuple-element.330, f32[2560,64]{1,0:T(8,128)S(1)} %gather_fusion, f32[2560,64]{1,0:T(8,128)S(1)} %get-tuple-element.313, pred[2560]{0:T(1024)(128)(4,1)S(1)} %get-tuple-element.293, ...), kind=kOutput, calls=%fused_computation.6.clone.1 | convolution fusion | flops 5033820160 | bytes 29496324 | tf_op jit(solution)/shard_map/while/body/eval_jaxpr/dot_general | solution.py:23
  494.8 40.6 %all-gather.13.cloned.1.call-done = f32[20480,64]{0,1:T(8,128)} async-done(((f32[2560,64]{0,1:T(8,128)}), f32[20480,64]{0,1:T(8,128)}) %all-gather.13.cloned.1.call-update) | async-done | bytes 5242896 | tf_op jit(solution)/shard_map/while/body/eval_jaxpr/all_gather | solution.py:13
  535.4 5.4 copy.33
  542.2 1.5 copy.34
  543.7 2.5 broadcast_select_fusion.6
  546.2 58.9 %all-reduce.5.cloned.1.call-done = f32[2560,64]{1,0:T(8,128)} async-done(((f32[2560,64]{1,0:T(8,128)}), f32[2560,64]{1,0:T(8,128)}) %all-reduce.5.cloned.1.call-update) | async-done | bytes 655376 | tf_op jit(solution)/shard_map/while/body/eval_jaxpr/psum | solution.py:9
  605.1 6.9 gather_fusion.1
  612.0 5.7 fusion.53
  617.8 29.3 %fusion.49 = f32[2560,64]{0,1:T(8,128)} fusion(f32[2,2560,2560]{2,1,0:T(8,128)} %get-tuple-element.329, s32[]{:T(128)S(6)} %select_n.295, f32[2560,64]{1,0:T(8,128)S(1)} %get-tuple-element.313, pred[]{:T(512)S(6)} %compare.37), kind=kOutput, calls=%fused_computation.4.clone.1 | convolution fusion | flops 5033328640 | bytes 27525124 | tf_op jit(solution)/shard_map/while/body/eval_jaxpr/dot_general | solution.py:23
  647.2 40.6 %all-gather.11.cloned.1.call-done = f32[20480,64]{0,1:T(8,128)} async-done(((f32[2560,64]{0,1:T(8,128)}), f32[20480,64]{0,1:T(8,128)}) %all-gather.11.cloned.1.call-update) | async-done | bytes 5242896 | tf_op jit(solution)/shard_map/while/body/eval_jaxpr/all_gather | solution.py:13
  687.8 5.4 copy.31
  693.3 1.3 bitcast_reduce_fusion.4
  696.3 60.1 %all-reduce.3.cloned.1.call-done = f32[2560,64]{1,0:T(8,128)} async-done(((f32[2560,64]{1,0:T(8,128)}), f32[2560,64]{1,0:T(8,128)}) %all-reduce.3.cloned.1.call-update) | async-done | bytes 655376 | tf_op jit(solution)/shard_map/while/body/eval_jaxpr/psum | solution.py:9
  756.4 5.5 gather_fusion
  761.9 32.4 %fusion.51 = f32[2560,64]{0,1:T(8,128)} fusion(f32[2,2560,2560]{2,1,0:T(8,128)} %get-tuple-element.329, s32[]{:T(128)S(6)} %select_n.293, f32[2560,64]{1,0:T(8,128)} %get-tuple-element.330, f32[2560,64]{1,0:T(8,128)S(1)} %gather_fusion, f32[2560,64]{1,0:T(8,128)S(1)} %get-tuple-element.313, pred[2560]{0:T(1024)(128)(4,1)S(1)} %get-tuple-element.293, ...), kind=kOutput, calls=%fused_computation.6.clone.1 | convolution fusion | flops 5033820160 | bytes 29496324 | tf_op jit(solution)/shard_map/while/body/eval_jaxpr/dot_general | solution.py:23
  794.4 40.6 %all-gather.13.cloned.1.call-done = f32[20480,64]{0,1:T(8,128)} async-done(((f32[2560,64]{0,1:T(8,128)}), f32[20480,64]{0,1:T(8,128)}) %all-gather.13.cloned.1.call-update) | async-done | bytes 5242896 | tf_op jit(solution)/shard_map/while/body/eval_jaxpr/all_gather | solution.py:13
  835.1 5.4 copy.33
  841.8 1.5 copy.34
  844.5 60.6 %all-reduce.5.cloned.1.call-done = f32[2560,64]{1,0:T(8,128)} async-done(((f32[2560,64]{1,0:T(8,128)}), f32[2560,64]{1,0:T(8,128)}) %all-reduce.5.cloned.1.call-update) | async-done | bytes 655376 | tf_op jit(solution)/shard_map/while/body/eval_jaxpr/psum | solution.py:9
  905.1 6.9 gather_fusion.1
  912.0 5.7 fusion.53
  917.8 29.3 %fusion.49 = f32[2560,64]{0,1:T(8,128)} fusion(f32[2,2560,2560]{2,1,0:T(8,128)} %get-tuple-element.329, s32[]{:T(128)S(6)} %select_n.295, f32[2560,64]{1,0:T(8,128)S(1)} %get-tuple-element.313, pred[]{:T(512)S(6)} %compare.37), kind=kOutput, calls=%fused_computation.4.clone.1 | convolution fusion | flops 5033328640 | bytes 27525124 | tf_op jit(solution)/shard_map/while/body/eval_jaxpr/dot_general | solution.py:23
  947.2 40.6 %all-gather.11.cloned.1.call-done = f32[20480,64]{0,1:T(8,128)} async-done(((f32[2560,64]{0,1:T(8,128)}), f32[20480,64]{0,1:T(8,128)}) %all-gather.11.cloned.1.call-update) | async-done | bytes 5242896 | tf_op jit(solution)/shard_map/while/body/eval_jaxpr/all_gather | solution.py:13
  987.9 5.4 copy.31
  996.4 60.1 %all-reduce.3.cloned.1.call-done = f32[2560,64]{1,0:T(8,128)} async-done(((f32[2560,64]{1,0:T(8,128)}), f32[2560,64]{1,0:T(8,128)}) %all-reduce.3.cloned.1.call-update) | async-done | bytes 655376 | tf_op jit(solution)/shard_map/while/body/eval_jaxpr/psum | solution.py:9
  1056.5 5.5 gather_fusion
  1061.9 32.4 %fusion.51 = f32[2560,64]{0,1:T(8,128)} fusion(f32[2,2560,2560]{2,1,0:T(8,128)} %get-tuple-element.329, s32[]{:T(128)S(6)} %select_n.293, f32[2560,64]{1,0:T(8,128)} %get-tuple-element.330, f32[2560,64]{1,0:T(8,128)S(1)} %gather_fusion, f32[2560,64]{1,0:T(8,128)S(1)} %get-tuple-element.313, pred[2560]{0:T(1024)(128)(4,1)S(1)} %get-tuple-element.293, ...), kind=kOutput, calls=%fused_computation.6.clone.1 | convolution fusion | flops 5033820160 | bytes 29496324 | tf_op jit(solution)/shard_map/while/body/eval_jaxpr/dot_general | solution.py:23
  1094.4 40.6 %all-gather.13.cloned.1.call-done = f32[20480,64]{0,1:T(8,128)} async-done(((f32[2560,64]{0,1:T(8,128)}), f32[20480,64]{0,1:T(8,128)}) %all-gather.13.cloned.1.call-update) | async-done | bytes 5242896 | tf_op jit(solution)/shard_map/while/body/eval_jaxpr/all_gather | solution.py:13
  1135.1 5.4 copy.33
  1141.9 1.5 copy.34
  1143.3 2.5 broadcast_select_fusion.6
  1145.9 58.9 %all-reduce.5.cloned.1.call-done = f32[2560,64]{1,0:T(8,128)} async-done(((f32[2560,64]{1,0:T(8,128)}), f32[2560,64]{1,0:T(8,128)}) %all-reduce.5.cloned.1.call-update) | async-done | bytes 655376 | tf_op jit(solution)/shard_map/while/body/eval_jaxpr/psum | solution.py:9
  1204.7 6.9 gather_fusion.1
  1211.6 5.7 fusion.53
  1217.6 10.8 gather_fusion.2
  1228.4 1.6 copy.17
  1229.9 2.3 broadcast_select_fusion.2
  1232.3 3.7 all-to-all-start.1
  1237.2 14.2 %all-to-all-done.1 = f32[8,512,64]{1,2,0:T(8,128)S(1)} async-done(((f32[8,512,64]{1,2,0:T(8,128)}), f32[8,512,64]{1,2,0:T(8,128)S(1)}, u32[]{:S(2)}, u32[]{:S(2)}) %all-to-all-start.1) | async-done | bytes 1048608 | tf_op jit(solution)/shard_map/all_to_all | solution.py:54
  1251.4 20.2 %fusion.32 = f32[1,1024,64]{1,2,0:T(8,128)} fusion(f32[1,1024,64]{1,2,0:T(8,128)S(1)} %copy-done, f32[4096,64]{0,1:T(8,128)S(1)} %bitcast.58, f32[1,1024,4096]{2,1,0:T(8,128)} %param.11), kind=kOutput, calls=%fused_computation.44 | convolution fusion | flops 3221291008 | bytes 18350080 | tf_op jit(solution)/shard_map/dot_general | solution.py:55
  (82 shorter events, 17.5 us)
Async XLA Ops:
  7.2 10.0 all-to-all-start
  18.4 1199.2 %copy-start.2 = (s32[4096]{0:T(1024)S(1)}, s32[4096]{0:T(1024)}, u32[]{:S(2)}) copy-start(s32[4096]{0:T(1024)} %broadcast_clamp_fusion) | copy-start | bytes 49156
  18.4 70.1 %all-gather.11.cloned.1.call-start = ((), (), s32[]{:S(2)}) async-start(), calls=%async_computation.2 | async-start | bytes 5898240 | tf_op jit(solution)/shard_map/while/body/eval_jaxpr/all_gather | solution.py:13
  47.7 109.3 %all-reduce.3.cloned.1.call-start = ((), (), s32[]{:S(2)}) async-start(), calls=%async_computation.3 | async-start | bytes 2621440 | tf_op jit(solution)/shard_map/while/body/eval_jaxpr/psum | solution.py:9
  96.8 138.7 %all-gather.13.cloned.1.call-start = ((), (), s32[]{:S(2)}) async-start(), calls=%async_computation.4 | async-start | bytes 5898240 | tf_op jit(solution)/shard_map/while/body/eval_jaxpr/all_gather | solution.py:13
  194.8 110.7 %all-reduce.5.cloned.1.call-start = ((), (), s32[]{:S(2)}) async-start(), calls=%async_computation.5 | async-start | bytes 2621440 | tf_op jit(solution)/shard_map/while/body/eval_jaxpr/psum | solution.py:9
  318.2 70.1 %all-gather.11.cloned.1.call-start = ((), (), s32[]{:S(2)}) async-start(), calls=%async_computation.2 | async-start | bytes 5898240 | tf_op jit(solution)/shard_map/while/body/eval_jaxpr/all_gather | solution.py:13
  347.6 109.3 %all-reduce.3.cloned.1.call-start = ((), (), s32[]{:S(2)}) async-start(), calls=%async_computation.3 | async-start | bytes 2621440 | tf_op jit(solution)/shard_map/while/body/eval_jaxpr/psum | solution.py:9
  396.7 138.7 %all-gather.13.cloned.1.call-start = ((), (), s32[]{:S(2)}) async-start(), calls=%async_computation.4 | async-start | bytes 5898240 | tf_op jit(solution)/shard_map/while/body/eval_jaxpr/all_gather | solution.py:13
  494.7 110.3 %all-reduce.5.cloned.1.call-start = ((), (), s32[]{:S(2)}) async-start(), calls=%async_computation.5 | async-start | bytes 2621440 | tf_op jit(solution)/shard_map/while/body/eval_jaxpr/psum | solution.py:9
  617.7 70.1 %all-gather.11.cloned.1.call-start = ((), (), s32[]{:S(2)}) async-start(), calls=%async_computation.2 | async-start | bytes 5898240 | tf_op jit(solution)/shard_map/while/body/eval_jaxpr/all_gather | solution.py:13
  647.1 109.3 %all-reduce.3.cloned.1.call-start = ((), (), s32[]{:S(2)}) async-start(), calls=%async_computation.3 | async-start | bytes 2621440 | tf_op jit(solution)/shard_map/while/body/eval_jaxpr/psum | solution.py:9
  696.2 138.9 %all-gather.13.cloned.1.call-start = ((), (), s32[]{:S(2)}) async-start(), calls=%async_computation.4 | async-start | bytes 5898240 | tf_op jit(solution)/shard_map/while/body/eval_jaxpr/all_gather | solution.py:13
  794.4 110.7 %all-reduce.5.cloned.1.call-start = ((), (), s32[]{:S(2)}) async-start(), calls=%async_computation.5 | async-start | bytes 2621440 | tf_op jit(solution)/shard_map/while/body/eval_jaxpr/psum | solution.py:9
  917.7 70.1 %all-gather.11.cloned.1.call-start = ((), (), s32[]{:S(2)}) async-start(), calls=%async_computation.2 | async-start | bytes 5898240 | tf_op jit(solution)/shard_map/while/body/eval_jaxpr/all_gather | solution.py:13
  947.2 109.3 %all-reduce.3.cloned.1.call-start = ((), (), s32[]{:S(2)}) async-start(), calls=%async_computation.3 | async-start | bytes 2621440 | tf_op jit(solution)/shard_map/while/body/eval_jaxpr/psum | solution.py:9
  996.2 138.9 %all-gather.13.cloned.1.call-start = ((), (), s32[]{:S(2)}) async-start(), calls=%async_computation.4 | async-start | bytes 5898240 | tf_op jit(solution)/shard_map/while/body/eval_jaxpr/all_gather | solution.py:13
  1094.4 110.3 %all-reduce.5.cloned.1.call-start = ((), (), s32[]{:S(2)}) async-start(), calls=%async_computation.5 | async-start | bytes 2621440 | tf_op jit(solution)/shard_map/while/body/eval_jaxpr/psum | solution.py:9
  1228.3 1.6 copy-start.1
  1232.3 19.0 %all-to-all-start.1 = ((f32[8,512,64]{1,2,0:T(8,128)}), f32[8,512,64]{1,2,0:T(8,128)S(1)}, u32[]{:S(2)}, u32[]{:S(2)}) async-start(f32[8,512,64]{1,2,0:T(8,128)} %broadcast_select_fusion.2), calls=%async_computation.1 | async-start | bytes 2097152 | tf_op jit(solution)/shard_map/all_to_all | solution.py:54
  1237.2 14.2 %copy-start = (f32[1,1024,64]{1,2,0:T(8,128)S(1)}, f32[1,1024,64]{1,2,0:T(8,128)}, u32[]{:S(2)}) copy-start(f32[1,1024,64]{1,2,0:T(8,128)} %param.12) | copy-start | bytes 786436
Sparse Core Ops, SparseCore 0:
  47.8 40.5 all-gather.10
  96.9 60.0 all-reduce.2
  194.9 40.5 all-gather.12
  245.0 60.4 all-reduce.4
  347.7 40.5 all-gather.10
  396.8 60.0 all-reduce.2
  494.8 40.5 all-gather.12
  546.3 58.7 all-reduce.4
  647.3 40.5 all-gather.10
  696.3 60.0 all-reduce.2
  794.5 40.5 all-gather.12
  844.6 60.4 all-reduce.4
  947.3 40.5 all-gather.10
  996.3 60.0 all-reduce.2
  1094.5 40.5 all-gather.12
  1145.9 58.7 all-reduce.4
